TPU v7x, 256 devices: a whole 4x4x8 slice. The times are simulated.
256 devices in a mesh: section: 64 (over z, x, core), blk: 4 (over y).
Axes of the slice: x: 4, y: 4, z: 8, core: 2. Of those that a mesh axis runs over, the one named last changes fastest.
Arguments:
- held_outputs: bfloat16 [64, 128, 12288], P('section', None, 'blk'), may hold values from -6 to 6
- held_cotangents: bfloat16 [64, 128, 12288], P('section', None, 'blk'), may hold values from -6 to 6
- new_rows: bfloat16 [2, 128, 12288], P(None, 'section', 'blk'), may hold values from -6 to 6
- targets: bfloat16 [2, 128, 12288], P(None, 'section', 'blk'), may hold values from -6 to 6
- saved_first: bfloat16 [64, 2, 128, 32, 384], P('section', None, None, None, 'blk'), may hold values from -6 to 6
- up_first: bfloat16 [64, 32, 384, 384], P('section', 'blk'), may hold values from -0.3125 to 0.3125
- up_second: bfloat16 [64, 384, 32, 128], P('section', 'blk'), may hold values from -1 to 1
- down_first: bfloat16 [64, 384, 32, 128], P('section', 'blk'), may hold values from -0.5 to 0.5
- down_second: bfloat16 [64, 32, 384, 384], P('section', 'blk'), may hold values from -0.3125 to 0.3125
Outputs:
- next_outputs: bfloat16 [64, 128, 12288], P('section', None, 'blk')
- next_cotangents: bfloat16 [64, 128, 12288], P('section', None, 'blk')
- grad_up_second: bfloat16 [64, 384, 32, 128], P('section', 'blk')
- grad_down_first: bfloat16 [64, 384, 32, 128], P('section', 'blk')
All inputs are finite; a program needn't handle non-finite values.
Results may differ from a plain program's by a relative error of at most 0.014.
Values may be sent and summed in bfloat16 or wider, within the bound.
A program may use at most 192 MiB of HBM per device.

v0:
```python
import functools

import jax
import jax.numpy as jnp
from jax import lax
from jax.experimental import pallas as pl
from jax.experimental.pallas import tpu as pltpu
from jax.sharding import PartitionSpec as P

BF = jnp.bfloat16
F32 = jnp.float32
MESH = pl.DeviceIdType.MESH
LANES = 128
TILE = 16
ROOT = 0.7978845608028654
CUBE = 0.044715


def contract(left, right, left_dim, right_dim):
    return lax.dot_general(
        left, right, (((left_dim,), (right_dim,)), ((), ())), preferred_element_type=F32
    )


def gelu_parts(value):
    square = value * value
    bent = jnp.tanh(ROOT * (value + CUBE * (square * value)))
    half = 0.5 * (1.0 + bent)
    return square, bent, half


def kernel(
    sections,
    parts,
    held_out,
    held_cot,
    rows_in,
    goals_in,
    saved_in,
    up_big_in,
    up_small_in,
    down_small_in,
    down_big_in,
    out_ref,
    cot_ref,
    grad_up_ref,
    grad_down_ref,
    up_big,
    down_big,
    up_small,
    down_small,
    up_turned,
    down_turned,
    kept,
    x_in,
    g_in,
    made_out,
    made_cot,
    sent,
    got,
    regrouped,
    staged,
    sum_up,
    sum_down,
    gathered,
    goals,
    swap,
    spread,
    load_sem,
    keep_sem,
    own_sem,
    gather_send,
    gather_recv,
    x_send,
    x_recv,
    g_send,
    g_recv,
    a_send,
    a_recv,
    store_sem,
):
    ticks, count, features = x_in.shape
    local_blocks, width = up_big.shape[0], up_big.shape[1]
    slab, all_blocks = up_small.shape[0], up_small.shape[1]
    groups = slab // TILE
    halves = all_blocks // TILE
    sec = lax.axis_index("section")
    blk = lax.axis_index("blk")
    last = sections - 1
    is_first = sec == 0
    is_last = sec == last

    barrier = pltpu.get_barrier_semaphore()

    def greet(s, b):
        pl.semaphore_signal(barrier, inc=1, device_id=(s, b), device_id_type=MESH)

    for k in range(1, parts):
        greet(sec, lax.rem(blk + k, parts))

    @pl.when(sec > 0)
    def _():
        greet(sec - 1, blk)

    @pl.when(sec < last)
    def _():
        greet(sec + 1, blk)

    for ends in (0, last):

        @pl.when(sec == ends)
        def _():
            def one(s, carry):
                @pl.when(s != ends)
                def _():
                    greet(s, blk)

                return carry

            lax.fori_loop(0, sections, one, 0)

    loads = [
        pltpu.make_async_copy(up_big_in, up_big, load_sem.at[0]),
        pltpu.make_async_copy(up_small_in, up_small, load_sem.at[1]),
        pltpu.make_async_copy(down_small_in, down_small, load_sem.at[2]),
        pltpu.make_async_copy(down_big_in, down_big, load_sem.at[3]),
    ]
    for load in loads:
        load.start()
    keeps = [
        pltpu.make_async_copy(saved_in.at[t], kept.at[t], keep_sem.at[t]) for t in range(ticks)
    ]
    for keep in keeps:
        keep.start()

    awaited = (parts - 1) + jnp.where(is_first, 0, 2) + jnp.where(is_last, 0, 2)
    pl.semaphore_wait(barrier, awaited)

    def to_end(t, which, end):
        piece = (rows_in, goals_in)[which]
        return pltpu.make_async_remote_copy(
            piece.at[t],
            gathered.at[t, sec],
            gather_send.at[t, which],
            gather_recv.at[t],
            device_id=(end, blk),
            device_id_type=MESH,
        )

    def at_end(t, which):
        piece = (rows_in, goals_in)[which]
        return pltpu.make_async_copy(piece.at[t], gathered.at[t, sec], own_sem.at[t])

    def shift(t, j, source, forward):
        column = pl.ds(pl.multiple_of(j * width, LANES), width)
        if forward:
            return pltpu.make_async_remote_copy(
                source.at[:, column],
                x_in.at[t, :, column],
                x_send.at[t],
                x_recv.at[t, j],
                device_id=(sec + 1, blk),
                device_id_type=MESH,
            )
        return pltpu.make_async_remote_copy(
            source.at[:, column],
            g_in.at[t, :, column],
            g_send.at[t],
            g_recv.at[t, j],
            device_id=(sec - 1, blk),
            device_id_type=MESH,
        )

    def send_ends(t):
        for which, end in ((0, 0), (1, last)):

            @pl.when(sec != end)
            def _():
                to_end(t, which, end).start()

            @pl.when(sec == end)
            def _():
                at_end(t, which).start()

    send_ends(0)

    def first_shift(j, carry):
        @pl.when(sec < last)
        def _():
            shift(0, j, held_out, True).start()

        return carry

    lax.fori_loop(0, local_blocks, first_shift, 0)

    def first_return(j, carry):
        @pl.when(sec > 0)
        def _():
            shift(0, j, held_cot, False).start()

        return carry

    lax.fori_loop(0, local_blocks, first_return, 0)
    for t in range(1, ticks):
        send_ends(t)

    side = TILE * TILE
    row = lax.broadcasted_iota(jnp.int32, (side, side), 0)
    col = lax.broadcasted_iota(jnp.int32, (side, side), 1)
    swap[...] = jnp.where(
        col == lax.rem(row, TILE) * TILE + lax.div(row, TILE), 1.0, 0.0
    ).astype(BF)
    per = count // sections
    tiles = TILE // per
    r_row = lax.rem(row, per)
    r_sec = lax.rem(lax.div(row, per), TILE)
    r_tile = lax.div(row, per * TILE)
    spread[...] = jnp.where(
        col == r_sec * TILE + r_tile * per + r_row, 1.0, 0.0
    ).astype(BF)

    def unpack(t, target):
        pltpu.make_async_remote_copy(
            gathered.at[t, pl.ds(0, sections - 1)],
            gathered.at[t, pl.ds(0, sections - 1)],
            gather_send.at[t, 0],
            gather_recv.at[t],
            device_id=(0, blk),
            device_id_type=MESH,
        ).wait_recv()
        pltpu.make_async_copy(rows_in.at[t], gathered.at[t, 0], own_sem.at[t]).wait()
        for a in range(sections // TILE):
            for b in range(features // LANES // tiles):
                chunk = gathered[
                    t, a * TILE : (a + 1) * TILE, b * TILE : (b + 1) * TILE, :
                ].reshape(side, LANES)
                moved = contract(spread[...], chunk, 1, 0).astype(BF)
                height = TILE * per
                for c in range(tiles):
                    lane = (b * tiles + c) * LANES
                    target[
                        t, a * height : (a + 1) * height, lane : lane + LANES
                    ] = moved[c * height : (c + 1) * height]

    for load in loads:
        load.wait()

    def turn(i, carry):
        up_turned[i] = up_small[i].T
        down_turned[i] = down_small[i].T
        return carry

    lax.fori_loop(0, slab, turn, 0, unroll=4)

    def peer(k):
        return lax.rem(blk + k, parts)

    def send_block(a, j):
        for k in (1, 3, 2):
            to = peer(k)
            pltpu.make_async_remote_copy(
                sent.at[a, to * local_blocks + j],
                got.at[a, blk * local_blocks + j],
                a_send.at[a, k],
                a_recv.at[a, k],
                device_id=(sec, to),
                device_id_type=MESH,
            ).start()

    def send_units(a, g):
        units = pl.ds(g * TILE, TILE)
        for k in (1, 3, 2):
            to = peer(k)
            pltpu.make_async_remote_copy(
                sent.at[a, pl.ds(to * local_blocks, local_blocks), units],
                got.at[a, pl.ds(blk * local_blocks, local_blocks), units],
                a_send.at[a, k],
                a_recv.at[a, k],
                device_id=(sec, to),
                device_id_type=MESH,
            ).start()

    def whole(a, k):
        to = peer(k)
        return pltpu.make_async_remote_copy(
            sent.at[a, pl.ds(to * local_blocks, local_blocks)],
            got.at[a, pl.ds(blk * local_blocks, local_blocks)],
            a_send.at[a, k],
            a_recv.at[a, k],
            device_id=(sec, to),
            device_id_type=MESH,
        )

    def arrive(a):
        for k in range(1, parts):
            whole(a, k).wait_recv()

    def put_block(a, j, value):
        for d in range(parts):
            sent[a, d * local_blocks + j] = value[d * slab : (d + 1) * slab]
        got[a, blk * local_blocks + j] = sent[a, blk * local_blocks + j]
        send_block(a, j)

    def block_of(a, j):
        return jnp.concatenate(
            [got[a, d * local_blocks + j] for d in range(parts)], axis=0
        )

    def units_in(a, g, also=None):
        units = pl.ds(g * TILE, TILE)
        for h in range(halves):
            chunk = got[a, h * TILE : (h + 1) * TILE, units, :].reshape(side, LANES)
            moved = contract(swap[...], chunk, 1, 0).astype(BF).reshape(TILE, TILE, LANES)
            regrouped[:, h * TILE : (h + 1) * TILE, :] = moved
            if also is not None:

                @pl.when(is_last)
                def _():
                    kept[also, units, h * TILE : (h + 1) * TILE, :] = moved

    def units_out(a, g):
        units = pl.ds(g * TILE, TILE)
        for h in range(halves):
            chunk = staged[:, h * TILE : (h + 1) * TILE, :].reshape(side, LANES)
            moved = contract(swap[...], chunk, 1, 0).astype(BF).reshape(TILE, TILE, LANES)
            sent[a, h * TILE : (h + 1) * TILE, units, :] = moved
        mine = pl.ds(blk * local_blocks, local_blocks)
        got[a, mine, units, :] = sent[a, mine, units, :]
        send_units(a, g)

    def forward_blocks(t, a):
        @pl.when(is_first)
        def _():
            unpack(t, x_in)

        def one(j, carry):
            @pl.when(sec > 0)
            def _():
                shift(t, j, held_out, True).wait_recv()

            column = pl.ds(pl.multiple_of(j * width, LANES), width)
            first = contract(x_in[t, :, column], up_big[j], 1, 0).astype(BF)
            put_block(a, j, first.T)
            return carry

        lax.fori_loop(0, local_blocks, one, 0)

    def forward_units(t, a, b):
        arrive(a)
        keeps[t].wait()

        def one(g, carry):
            units_in(a, g, t)
            for u in range(TILE):
                i = g * TILE + u
                pre = contract(up_turned[i], regrouped[u], 1, 0)
                square, bent, half = gelu_parts(pre)
                act = (pre * half).astype(BF)
                staged[u] = contract(down_small[i], act, 1, 0).astype(BF)
            units_out(b, g)
            return carry

        lax.fori_loop(0, groups, one, 0)

    def forward_out(t, b):
        arrive(b)

        @pl.when(is_last)
        def _():
            unpack(t, goals)

        def one(j, carry):
            column = pl.ds(pl.multiple_of(j * width, LANES), width)
            branch = contract(block_of(b, j), down_big[j], 0, 0)
            made = (x_in[t, :, column].astype(F32) + branch).astype(BF)
            made_out[t, :, column] = made
            if t + 1 < ticks:

                @pl.when(sec < last)
                def _():
                    shift(t + 1, j, made_out.at[t], True).start()

            @pl.when(is_last)
            def _():
                g_in[t, :, column] = (
                    made.astype(F32) - goals[t, :, column].astype(F32)
                ).astype(BF)

            return carry

        lax.fori_loop(0, local_blocks, one, 0)

    def backward_blocks(t, a):
        def one(j, carry):
            @pl.when(sec < last)
            def _():
                shift(t, j, held_cot, False).wait_recv()

            column = pl.ds(pl.multiple_of(j * width, LANES), width)
            back = contract(down_big[j], g_in[t, :, column], 1, 1).astype(BF)
            put_block(a, j, back)
            return carry

        lax.fori_loop(0, local_blocks, one, 0)

    def backward_units(t, a, b):
        arrive(a)

        def one(g, carry):
            units_in(a, g)
            for u in range(TILE):
                i = g * TILE + u
                held = kept[t, i]
                mixed = regrouped[u]
                pre = contract(up_turned[i], held, 1, 0)
                back_act = contract(down_turned[i], mixed, 1, 0)
                square, bent, half = gelu_parts(pre)
                act = (pre * half).astype(BF)
                slope = half + (0.5 * ROOT) * pre * (1.0 - bent * bent) * (
                    1.0 + (3.0 * CUBE) * square
                )
                back_pre = (back_act * slope).astype(BF)
                staged[u] = contract(up_small[i], back_pre, 1, 0).astype(BF)
                grad_up = contract(held, back_pre, 1, 1)
                grad_down = contract(mixed, act, 1, 1)
                if t == 0:
                    sum_up[i] = grad_up
                    sum_down[i] = grad_down
                elif t + 1 < ticks:
                    sum_up[i] += grad_up
                    sum_down[i] += grad_down
                else:
                    up_turned_out = (sum_up[i] + grad_up).astype(BF)
                    down_turned_out = (sum_down[i] + grad_down).astype(BF)
                    kept[0, i] = up_turned_out
                    kept[t, i] = down_turned_out
            units_out(b, g)
            return carry

        lax.fori_loop(0, groups, one, 0)

    def backward_out(t, b):
        arrive(b)

        def one(j, carry):
            column = pl.ds(pl.multiple_of(j * width, LANES), width)
            back_in = contract(block_of(b, j), up_big[j], 0, 1)
            made_cot[t, :, column] = (
                g_in[t, :, column].astype(F32) + back_in
            ).astype(BF)
            if t + 1 < ticks:

                @pl.when(sec > 0)
                def _():
                    shift(t + 1, j, made_cot.at[t], False).start()

            return carry

        lax.fori_loop(0, local_blocks, one, 0)

    end = ticks - 1
    forward_blocks(0, 0)
    forward_units(0, 0, 1)
    forward_out(0, 1)
    for t in range(ticks):
        backward_blocks(t, 4 * t + 2)
        if t < end:
            forward_blocks(t + 1, 4 * t + 4)
        backward_units(t, 4 * t + 2, 4 * t + 3)
        if t == end:
            stores = [
                pltpu.make_async_copy(kept.at[0], grad_up_ref, store_sem.at[1]),
                pltpu.make_async_copy(kept.at[end], grad_down_ref, store_sem.at[2]),
            ]
            for store in stores:
                store.start()
        if t < end:
            forward_units(t + 1, 4 * t + 4, 4 * t + 5)
        backward_out(t, 4 * t + 3)
        if t < end:
            forward_out(t + 1, 4 * t + 5)
            if t + 1 == end:
                stored_out = pltpu.make_async_copy(made_out.at[end], out_ref, store_sem.at[0])
                stored_out.start()
    stored_cot = pltpu.make_async_copy(made_cot.at[end], cot_ref, store_sem.at[3])
    stored_cot.start()

    for t in range(ticks):
        for which, far in ((0, 0), (1, last)):

            @pl.when(sec != far)
            def _():
                to_end(t, which, far).wait_send()

        @pl.when(sec < last)
        def _():
            pltpu.make_async_remote_copy(
                made_out.at[0],
                x_in.at[t],
                x_send.at[t],
                x_recv.at[t, 0],
                device_id=(sec + 1, blk),
                device_id_type=MESH,
            ).wait_send()

        @pl.when(sec > 0)
        def _():
            pltpu.make_async_remote_copy(
                made_cot.at[0],
                g_in.at[t],
                g_send.at[t],
                g_recv.at[t, 0],
                device_id=(sec - 1, blk),
                device_id_type=MESH,
            ).wait_send()

    for a in range(4 * ticks):
        for k in range(1, parts):
            whole(a, k).wait_send()
    for store in stores:
        store.wait()
    stored_out.wait()
    stored_cot.wait()


def local(
    held_outputs,
    held_cotangents,
    new_rows,
    targets,
    saved_first,
    up_first,
    up_second,
    down_first,
    down_second,
):
    sections = lax.axis_size("section")
    parts = lax.axis_size("blk")
    count, features = held_outputs.shape[1:]
    ticks, per = new_rows.shape[:2]
    local_blocks, width = up_first.shape[1:3]
    slab, all_blocks, hidden = up_second.shape[1:]
    exchanges = 4 * ticks

    def piece(rows):
        tiles = rows.reshape(ticks, per, features // LANES, LANES)
        return tiles.transpose(0, 2, 1, 3).reshape(ticks, per * features // LANES, LANES)

    saved = saved_first[0].transpose(0, 3, 2, 1)
    anywhere = pl.BlockSpec(memory_space=pl.ANY)
    vmem = pltpu.VMEM
    dma = pltpu.SemaphoreType.DMA
    outs = pl.pallas_call(
        functools.partial(kernel, sections, parts),
        out_shape=(
            jax.ShapeDtypeStruct((count, features), BF),
            jax.ShapeDtypeStruct((count, features), BF),
            jax.ShapeDtypeStruct((slab, all_blocks, hidden), BF),
            jax.ShapeDtypeStruct((slab, all_blocks, hidden), BF),
        ),
        in_specs=[anywhere] * 9,
        out_specs=(anywhere,) * 4,
        scratch_shapes=[
            vmem((local_blocks, width, width), BF),
            vmem((local_blocks, width, width), BF),
            vmem((slab, all_blocks, hidden), BF),
            vmem((slab, all_blocks, hidden), BF),
            vmem((slab, hidden, all_blocks), BF),
            vmem((slab, hidden, all_blocks), BF),
            vmem((ticks, slab, all_blocks, count), BF),
            vmem((ticks, count, features), BF),
            vmem((ticks, count, features), BF),
            vmem((ticks, count, features), BF),
            vmem((ticks, count, features), BF),
            vmem((exchanges, all_blocks, slab, count), BF),
            vmem((exchanges, all_blocks, slab, count), BF),
            vmem((TILE, all_blocks, count), BF),
            vmem((TILE, all_blocks, count), BF),
            vmem((slab, all_blocks, hidden), F32),
            vmem((slab, all_blocks, hidden), F32),
            vmem((ticks, sections, per * features // LANES, LANES), BF),
            vmem((ticks, count, features), BF),
            vmem((TILE * TILE, TILE * TILE), BF),
            vmem((TILE * TILE, TILE * TILE), BF),
            dma((4,)),
            dma((ticks,)),
            dma((ticks,)),
            dma((ticks, 2)),
            dma((ticks,)),
            dma((ticks,)),
            dma((ticks, local_blocks)),
            dma((ticks,)),
            dma((ticks, local_blocks)),
            dma((exchanges, parts)),
            dma((exchanges, parts)),
            dma((4,)),
        ],
        compiler_params=pltpu.CompilerParams(
            collective_id=0, has_side_effects=True, vmem_limit_bytes=60 * 1024 * 1024
        ),
        name="relay_window",
    )(
        held_outputs[0],
        held_cotangents[0],
        piece(new_rows),
        piece(targets),
        saved,
        up_first[0],
        up_second[0],
        down_first[0],
        down_second[0],
    )
    return tuple(out[None] for out in outs)


def solution(mesh):
    placed = (
        P("section", None, "blk"),
        P("section", None, "blk"),
        P(None, "section", "blk"),
        P(None, "section", "blk"),
        P("section", None, None, None, "blk"),
        P("section", "blk", None, None),
        P("section", "blk", None, None),
        P("section", "blk", None, None),
        P("section", "blk", None, None),
    )
    return jax.shard_map(
        local,
        mesh=mesh,
        in_specs=placed,
        out_specs=(
            P("section", None, "blk"),
            P("section", None, "blk"),
            P("section", "blk", None, None),
            P("section", "blk", None, None),
        ),
        check_vma=False,
    )
```

profile of v0, /device:TPU:6, one launch (start us, length us, event | category | flops | bytes accessed | tf_op | source)
XLA Modules:
  0.0 156.7 jit_solution(15392179067306178568)
XLA Ops:
  0.6 3.2 %copy.17 = bf16[1,2,128,32,96]{2,3,4,1,0:T(8,128)(2,1)} copy(bf16[1,2,128,32,96]{2,4,3,1,0:T(8,128)(2,1)} %param.13) | data formatting | bytes 3145728 | tf_op args[4]
  3.8 146.9 %relay_window.1 = (bf16[128,3072]{1,0:T(8,128)(2,1)}, bf16[128,3072]{1,0:T(8,128)(2,1)}, bf16[96,32,128]{2,1,0:T(8,128)(2,1)}, bf16[96,32,128]{2,1,0:T(8,128)(2,1)}) custom-call(bf16[128,3072]{1,0:T(8,128)(2,1)} %bitcast.28, bf16[128,3072]{1,0:T(8,128)(2,1)} %bitcast.29, bf16[2,48,128]{2,1,0:T(8,128)(2,1)} %bitcast.36, bf16[2,48,128]{2,1,0:T(8,128)(2,1)} %bitcast.37, ...), custom_call_target="tpu_custom_call" | custom-call | tf_op jit(solution)/shard_map/relay_window/pallas_call | solution.py:553
  150.7 0.0 copy-start.1
  150.7 0.0 copy-start
  150.7 2.2 %copy.22 = bf16[1,128,3072]{2,1,0:T(8,128)(2,1)} copy(bf16[1,128,3072]{2,1,0:T(8,128)(2,1)} %bitcast.35) | data formatting | bytes 1572864
  152.9 2.1 %copy.23 = bf16[1,128,3072]{2,1,0:T(8,128)(2,1)} copy(bf16[1,128,3072]{2,1,0:T(8,128)(2,1)} %bitcast.34) | data formatting | bytes 1572864
  154.9 0.0 copy-done.1
  155.0 0.9 copy.24
  155.8 0.0 copy-done
  155.8 0.9 copy.25
Async XLA Ops:
  150.7 4.3 %copy-start.1 = (bf16[96,32,128]{2,1,0:T(8,128)(2,1)S(1)}, bf16[96,32,128]{2,1,0:T(8,128)(2,1)}, u32[]{:S(2)}) copy-start(bf16[96,32,128]{2,1,0:T(8,128)(2,1)} %get-tuple-element.10) | copy-start | bytes 2359300
  150.7 5.1 %copy-start = (bf16[96,32,128]{2,1,0:T(8,128)(2,1)S(1)}, bf16[96,32,128]{2,1,0:T(8,128)(2,1)}, u32[]{:S(2)}) copy-start(bf16[96,32,128]{2,1,0:T(8,128)(2,1)} %get-tuple-element.11) | copy-start | bytes 2359300
where the time goes:
time: 157 us
  Pallas kernels  147 us (94%)
  local copies, waits for them, and re-layouts  9.2 us (6%)
    pallas_call x1, Pallas kernels, local(): pl.pallas_call(functools.partial(kernel, sections, parts), out_shape=(jax...  147 us
    unnamed x9, local copies, waits for them, and re-layouts  9.2 us

commit v1 on v0

--- a/solution.py
+++ b/solution.py
@@ -89,6 +89,8 @@
     last = sections - 1
     is_first = sec == 0
     is_last = sec == last
+    is_even = lax.rem(sec, 2) == 0
+    is_odd = jnp.logical_not(jnp.logical_or(is_even, is_last))
 
     barrier = pltpu.get_barrier_semaphore()
 
@@ -125,13 +127,38 @@
         pltpu.make_async_copy(down_small_in, down_small, load_sem.at[2]),
         pltpu.make_async_copy(down_big_in, down_big, load_sem.at[3]),
     ]
-    for load in loads:
-        load.start()
+    for k in (1, 2, 0, 3):
+        loads[k].start()
     keeps = [
         pltpu.make_async_copy(saved_in.at[t], kept.at[t], keep_sem.at[t]) for t in range(ticks)
     ]
     for keep in keeps:
         keep.start()
+
+    side = TILE * TILE
+    row = lax.broadcasted_iota(jnp.int32, (side, side), 0)
+    col = lax.broadcasted_iota(jnp.int32, (side, side), 1)
+    swap[...] = jnp.where(
+        col == lax.rem(row, TILE) * TILE + lax.div(row, TILE), 1.0, 0.0
+    ).astype(BF)
+    per = count // sections
+    tiles = TILE // per
+    r_row = lax.rem(row, per)
+    r_sec = lax.rem(lax.div(row, per), TILE)
+    r_tile = lax.div(row, per * TILE)
+    spread[...] = jnp.where(
+        col == r_sec * TILE + r_tile * per + r_row, 1.0, 0.0
+    ).astype(BF)
+
+    for load in loads[1:3]:
+        load.wait()
+
+    def turn(i, carry):
+        up_turned[i] = up_small[i].T
+        down_turned[i] = down_small[i].T
+        return carry
+
+    lax.fori_loop(0, slab, turn, 0, unroll=4)
 
     awaited = (parts - 1) + jnp.where(is_first, 0, 2) + jnp.where(is_last, 0, 2)
     pl.semaphore_wait(barrier, awaited)
@@ -203,21 +230,6 @@
     lax.fori_loop(0, local_blocks, first_return, 0)
     for t in range(1, ticks):
         send_ends(t)
-
-    side = TILE * TILE
-    row = lax.broadcasted_iota(jnp.int32, (side, side), 0)
-    col = lax.broadcasted_iota(jnp.int32, (side, side), 1)
-    swap[...] = jnp.where(
-        col == lax.rem(row, TILE) * TILE + lax.div(row, TILE), 1.0, 0.0
-    ).astype(BF)
-    per = count // sections
-    tiles = TILE // per
-    r_row = lax.rem(row, per)
-    r_sec = lax.rem(lax.div(row, per), TILE)
-    r_tile = lax.div(row, per * TILE)
-    spread[...] = jnp.where(
-        col == r_sec * TILE + r_tile * per + r_row, 1.0, 0.0
-    ).astype(BF)
 
     def unpack(t, target):
         pltpu.make_async_remote_copy(
@@ -242,15 +254,10 @@
                         t, a * height : (a + 1) * height, lane : lane + LANES
                     ] = moved[c * height : (c + 1) * height]
 
-    for load in loads:
-        load.wait()
-
-    def turn(i, carry):
-        up_turned[i] = up_small[i].T
-        down_turned[i] = down_small[i].T
-        return carry
-
-    lax.fori_loop(0, slab, turn, 0, unroll=4)
+    loads[0].wait()
+    loads[3].wait()
+    for keep in keeps:
+        keep.wait()
 
     def peer(k):
         return lax.rem(blk + k, parts)
@@ -306,17 +313,12 @@
             [got[a, d * local_blocks + j] for d in range(parts)], axis=0
         )
 
-    def units_in(a, g, also=None):
+    def units_in(a, g):
         units = pl.ds(g * TILE, TILE)
         for h in range(halves):
             chunk = got[a, h * TILE : (h + 1) * TILE, units, :].reshape(side, LANES)
             moved = contract(swap[...], chunk, 1, 0).astype(BF).reshape(TILE, TILE, LANES)
             regrouped[:, h * TILE : (h + 1) * TILE, :] = moved
-            if also is not None:
-
-                @pl.when(is_last)
-                def _():
-                    kept[also, units, h * TILE : (h + 1) * TILE, :] = moved
 
     def units_out(a, g):
         units = pl.ds(g * TILE, TILE)
@@ -347,10 +349,9 @@
 
     def forward_units(t, a, b):
         arrive(a)
-        keeps[t].wait()
 
         def one(g, carry):
-            units_in(a, g, t)
+            units_in(a, g)
             for u in range(TILE):
                 i = g * TILE + u
                 pre = contract(up_turned[i], regrouped[u], 1, 0)
@@ -358,6 +359,11 @@
                 act = (pre * half).astype(BF)
                 staged[u] = contract(down_small[i], act, 1, 0).astype(BF)
             units_out(b, g)
+
+            @pl.when(is_last)
+            def _():
+                kept[t, pl.ds(g * TILE, TILE)] = regrouped[...]
+
             return carry
 
         lax.fori_loop(0, groups, one, 0)
@@ -459,31 +465,56 @@
         lax.fori_loop(0, local_blocks, one, 0)
 
     end = ticks - 1
-    forward_blocks(0, 0)
-    forward_units(0, 0, 1)
-    forward_out(0, 1)
+    stores = [
+        pltpu.make_async_copy(made_out.at[end], out_ref, store_sem.at[0]),
+        pltpu.make_async_copy(kept.at[0], grad_up_ref, store_sem.at[1]),
+        pltpu.make_async_copy(kept.at[end], grad_down_ref, store_sem.at[2]),
+        pltpu.make_async_copy(made_cot.at[end], cot_ref, store_sem.at[3]),
+    ]
+
+    def stage(kind, t):
+        a = 4 * t
+        if kind == "FB":
+            forward_blocks(t, a)
+        elif kind == "FU":
+            forward_units(t, a, a + 1)
+        elif kind == "FO":
+            forward_out(t, a + 1)
+            if t == end:
+                stores[0].start()
+        elif kind == "BB":
+            backward_blocks(t, a + 2)
+        elif kind == "BU":
+            backward_units(t, a + 2, a + 3)
+            if t == end:
+                stores[1].start()
+                stores[2].start()
+        else:
+            backward_out(t, a + 3)
+            if t == end:
+                stores[3].start()
+
+    def only(who, *steps):
+        @pl.when(who)
+        def _():
+            for kind, t in steps:
+                stage(kind, t)
+
     for t in range(ticks):
-        backward_blocks(t, 4 * t + 2)
-        if t < end:
-            forward_blocks(t + 1, 4 * t + 4)
-        backward_units(t, 4 * t + 2, 4 * t + 3)
-        if t == end:
-            stores = [
-                pltpu.make_async_copy(kept.at[0], grad_up_ref, store_sem.at[1]),
-                pltpu.make_async_copy(kept.at[end], grad_down_ref, store_sem.at[2]),
-            ]
-            for store in stores:
-                store.start()
-        if t < end:
-            forward_units(t + 1, 4 * t + 4, 4 * t + 5)
-        backward_out(t, 4 * t + 3)
-        if t < end:
-            forward_out(t + 1, 4 * t + 5)
-            if t + 1 == end:
-                stored_out = pltpu.make_async_copy(made_out.at[end], out_ref, store_sem.at[0])
-                stored_out.start()
-    stored_cot = pltpu.make_async_copy(made_cot.at[end], cot_ref, store_sem.at[3])
-    stored_cot.start()
+        early, late = (is_even, is_odd) if t % 2 == 0 else (is_odd, is_even)
+        only(early, ("BB", t))
+        stage("FB", t)
+        if t > 0:
+            only(is_last, ("BO", t - 1))
+        only(late, ("BB", t))
+        only(early, ("BU", t))
+        stage("FU", t)
+        only(late, ("BU", t))
+        only(early, ("BO", t))
+        stage("FO", t)
+        only(late, ("BO", t))
+        only(is_last, ("BB", t), ("BU", t))
+    only(is_last, ("BO", end))
 
     for t in range(ticks):
         for which, far in ((0, 0), (1, last)):
@@ -519,8 +550,6 @@
             whole(a, k).wait_send()
     for store in stores:
         store.wait()
-    stored_out.wait()
-    stored_cot.wait()
 
 
 def local(

time: 157 us -> 147 us (0.936)
  the two profiles are of different devices: /device:TPU:6 before, /device:TPU:231 now
where the time goes in v1:
time: 147 us; the launch traced here: 146 us
  Pallas kernels  137 us (93%)
  local copies, waits for them, and re-layouts  9.2 us (6%)
    pallas_call x1, Pallas kernels, local(): pl.pallas_call(functools.partial(kernel, sections, parts), out_shape=(jax...  137 us
    unnamed x9, local copies, waits for them, and re-layouts  9.2 us

profile of v1, /device:TPU:231, one launch (start us, length us, event | category | flops | bytes accessed | tf_op | source)
XLA Modules:
  0.0 146.4 jit_solution(1813129823663297130)
XLA Ops:
  0.6 3.2 %copy.17 = bf16[1,2,128,32,96]{2,3,4,1,0:T(8,128)(2,1)} copy(bf16[1,2,128,32,96]{2,4,3,1,0:T(8,128)(2,1)} %param.13) | data formatting | bytes 3145728 | tf_op args[4]
  3.8 136.6 %relay_window.1 = (bf16[128,3072]{1,0:T(8,128)(2,1)}, bf16[128,3072]{1,0:T(8,128)(2,1)}, bf16[96,32,128]{2,1,0:T(8,128)(2,1)}, bf16[96,32,128]{2,1,0:T(8,128)(2,1)}) custom-call(bf16[128,3072]{1,0:T(8,128)(2,1)} %bitcast.28, bf16[128,3072]{1,0:T(8,128)(2,1)} %bitcast.29, bf16[2,48,128]{2,1,0:T(8,128)(2,1)} %bitcast.36, bf16[2,48,128]{2,1,0:T(8,128)(2,1)} %bitcast.37, ...), custom_call_target="tpu_custom_call" | custom-call | tf_op jit(solution)/shard_map/relay_window/pallas_call | solution.py:582
  140.4 0.0 copy-start.1
  140.4 0.0 copy-start
  140.4 2.2 %copy.22 = bf16[1,128,3072]{2,1,0:T(8,128)(2,1)} copy(bf16[1,128,3072]{2,1,0:T(8,128)(2,1)} %bitcast.35) | data formatting | bytes 1572864
  142.6 2.1 %copy.23 = bf16[1,128,3072]{2,1,0:T(8,128)(2,1)} copy(bf16[1,128,3072]{2,1,0:T(8,128)(2,1)} %bitcast.34) | data formatting | bytes 1572864
  144.7 0.0 copy-done.1
  144.7 0.9 copy.24
  145.6 0.0 copy-done
  145.6 0.9 copy.25
Async XLA Ops:
  140.4 4.3 %copy-start.1 = (bf16[96,32,128]{2,1,0:T(8,128)(2,1)S(1)}, bf16[96,32,128]{2,1,0:T(8,128)(2,1)}, u32[]{:S(2)}) copy-start(bf16[96,32,128]{2,1,0:T(8,128)(2,1)} %get-tuple-element.10) | copy-start | bytes 2359300
  140.4 5.1 %copy-start = (bf16[96,32,128]{2,1,0:T(8,128)(2,1)S(1)}, bf16[96,32,128]{2,1,0:T(8,128)(2,1)}, u32[]{:S(2)}) copy-start(bf16[96,32,128]{2,1,0:T(8,128)(2,1)} %get-tuple-element.11) | copy-start | bytes 2359300

commit v2 on v1

--- a/solution.py
+++ b/solution.py
@@ -352,12 +352,16 @@
 
         def one(g, carry):
             units_in(a, g)
-            for u in range(TILE):
+
+            def unit(u, carry):
                 i = g * TILE + u
                 pre = contract(up_turned[i], regrouped[u], 1, 0)
                 square, bent, half = gelu_parts(pre)
                 act = (pre * half).astype(BF)
                 staged[u] = contract(down_small[i], act, 1, 0).astype(BF)
+                return carry
+
+            lax.fori_loop(0, TILE, unit, 0, unroll=4)
             units_out(b, g)
 
             @pl.when(is_last)

time: 147 us -> 132 us (0.90)
  Pallas kernels: 137 us -> 122 us
    pallas_call x1, Pallas kernels: 137 us -> 122 us  [local(): pl.pallas_call(functools.partial(kernel, sections, parts), out_shape=(jax...]
where the time goes in v2:
time: 132 us
  Pallas kernels  122 us (92%)
  local copies, waits for them, and re-layouts  9.2 us (7%)
    pallas_call x1, Pallas kernels, local(): pl.pallas_call(functools.partial(kernel, sections, parts), out_shape=(jax...  122 us
    unnamed x9, local copies, waits for them, and re-layouts  9.2 us

profile of v2, /device:TPU:231, one launch (start us, length us, event | category | flops | bytes accessed | tf_op | source)
XLA Modules:
  0.0 132.1 jit_solution(6453199454898321199)
XLA Ops:
  0.6 3.2 %copy.17 = bf16[1,2,128,32,96]{2,3,4,1,0:T(8,128)(2,1)} copy(bf16[1,2,128,32,96]{2,4,3,1,0:T(8,128)(2,1)} %param.13) | data formatting | bytes 3145728 | tf_op args[4]
  3.8 122.3 %relay_window.1 = (bf16[128,3072]{1,0:T(8,128)(2,1)}, bf16[128,3072]{1,0:T(8,128)(2,1)}, bf16[96,32,128]{2,1,0:T(8,128)(2,1)}, bf16[96,32,128]{2,1,0:T(8,128)(2,1)}) custom-call(bf16[128,3072]{1,0:T(8,128)(2,1)} %bitcast.28, bf16[128,3072]{1,0:T(8,128)(2,1)} %bitcast.29, bf16[2,48,128]{2,1,0:T(8,128)(2,1)} %bitcast.36, bf16[2,48,128]{2,1,0:T(8,128)(2,1)} %bitcast.37, ...), custom_call_target="tpu_custom_call" | custom-call | tf_op jit(solution)/shard_map/relay_window/pallas_call | solution.py:586
  126.1 0.0 copy-start.1
  126.1 0.0 copy-start
  126.1 2.2 %copy.22 = bf16[1,128,3072]{2,1,0:T(8,128)(2,1)} copy(bf16[1,128,3072]{2,1,0:T(8,128)(2,1)} %bitcast.35) | data formatting | bytes 1572864
  128.3 2.1 %copy.23 = bf16[1,128,3072]{2,1,0:T(8,128)(2,1)} copy(bf16[1,128,3072]{2,1,0:T(8,128)(2,1)} %bitcast.34) | data formatting | bytes 1572864
  130.4 0.0 copy-done.1
  130.4 0.9 copy.24
  131.2 0.0 copy-done
  131.2 0.9 copy.25
Async XLA Ops:
  126.1 4.3 %copy-start.1 = (bf16[96,32,128]{2,1,0:T(8,128)(2,1)S(1)}, bf16[96,32,128]{2,1,0:T(8,128)(2,1)}, u32[]{:S(2)}) copy-start(bf16[96,32,128]{2,1,0:T(8,128)(2,1)} %get-tuple-element.10) | copy-start | bytes 2359300
  126.1 5.1 %copy-start = (bf16[96,32,128]{2,1,0:T(8,128)(2,1)S(1)}, bf16[96,32,128]{2,1,0:T(8,128)(2,1)}, u32[]{:S(2)}) copy-start(bf16[96,32,128]{2,1,0:T(8,128)(2,1)} %get-tuple-element.11) | copy-start | bytes 2359300
